TPU v7x, 1024 devices: a whole 4x4x32 slice. The times are simulated.
1024 devices in a mesh: ctx: 128 (over y, z), head: 8 (over x, core).
Axes of the slice: x: 4, y: 4, z: 32, core: 2. Of those that a mesh axis runs over, the one named last changes fastest.
Arguments:
- queries: bfloat16 [32768, 6144], P(('ctx', 'head')), may hold values from -120 to 120
- keys: bfloat16 [32768, 1024], P(('ctx', 'head')), may hold values from -6 to 6
- values: bfloat16 [32768, 1024], P(('ctx', 'head')), may hold values from -6 to 6
- outputs: bfloat16 [32768, 6144], P(('ctx', 'head')), may hold values from -6 to 6
- out_grad: bfloat16 [32768, 6144], P(('ctx', 'head')), may hold values from -6 to 6
- frame_lists: int32 [128, 5], P('ctx'), may hold values from -1 to 127, as said below
Outputs:
- grad_queries: bfloat16 [32768, 6144], P('ctx', 'head')
- key_gradient: bfloat16 [32768, 1024], P('ctx', 'head')
- value_gradient: bfloat16 [32768, 1024], P('ctx', 'head')
Inputs may be any that keep to these rules, and one draw needn't show every extreme that they name: `frame_lists`: entry o of the list of query frame f is f - o or -1 (always -1 where f - o < 0); entry 0 is f; entry 4 is f - 4 for every frame f divisible by 3 with f >= 4.
All inputs are finite; a program needn't handle non-finite values.
Results may differ from a plain program's by a relative error of at most 0.005.
Values may be sent and summed in bfloat16 or wider, within the bound.
No kernel may reach another device: no remote copies, remote signals or barrier semaphores. Data moves between devices by JAX's collectives and lax.ppermute only.
A program may use at most 32 MiB of HBM per device.

v0:
```python
import jax
import jax.numpy as jnp
from jax import lax
from jax.sharding import PartitionSpec as P

HEAD_SIZE = 128
FRAME = 256
REACH = 4


def passed_along(value, axis, steps):
    count = lax.axis_size(axis)
    initial, last = (max(0, -steps), min(count, count - steps))
    return lax.ppermute(value, axis, [(source, source + steps) for source in range(initial, last)])


def on_device(queries, keys, values, outputs, out_grad, frame_lists):
    q_loc, k_loc, v_loc, o_loc, g_loc = (
        lax.all_to_all(queries, "head", split_axis=1, concat_axis=0, tiled=True),
        lax.all_to_all(keys, "head", split_axis=1, concat_axis=0, tiled=True),
        lax.all_to_all(values, "head", split_axis=1, concat_axis=0, tiled=True),
        lax.all_to_all(outputs, "head", split_axis=1, concat_axis=0, tiled=True),
        lax.all_to_all(out_grad, "head", split_axis=1, concat_axis=0, tiled=True),
    )
    row_count = q_loc.shape[0]
    head_count = q_loc.shape[1] // HEAD_SIZE
    row_delta = jnp.sum(
        (g_loc.astype(jnp.float32) * o_loc.astype(jnp.float32)).reshape(
            row_count, head_count, HEAD_SIZE
        ),
        axis=2,
    )
    kv_count = k_loc.shape[1] // HEAD_SIZE
    query_group_width = head_count // kv_count
    reach_devs = REACH
    score_scaling = HEAD_SIZE ** (-0.5)
    dev_index = lax.axis_index("ctx")
    arrived = [
        passed_along((k_loc, v_loc), "ctx", distance) for distance in range(reach_devs, 0, -1)
    ]
    key_all = jnp.concatenate([piece[0] for piece in arrived] + [k_loc], axis=0)
    value_all = jnp.concatenate([piece[1] for piece in arrived] + [v_loc], axis=0)
    key_extent = key_all.shape[0]
    key_tok = (dev_index - reach_devs) * row_count + jnp.arange(key_extent, dtype=jnp.int32)
    key_frame = jnp.floor_divide(key_tok, FRAME)
    listed = (
        jnp.any(frame_lists[:, :, None] == key_frame[None, None, :], axis=1)
        & (key_tok >= 0)[None, :]
    )
    allowed = jnp.repeat(listed, FRAME, axis=0)
    query_heads = q_loc.reshape(row_count, head_count, HEAD_SIZE).transpose(1, 0, 2)
    grad_heads = g_loc.reshape(row_count, head_count, HEAD_SIZE).transpose(1, 0, 2)
    key_heads = key_all.reshape(key_extent, kv_count, HEAD_SIZE).transpose(1, 0, 2)
    value_heads = value_all.reshape(key_extent, kv_count, HEAD_SIZE).transpose(1, 0, 2)
    contract_last = (((1,), (1,)), ((), ()))
    contract_first = (((0,), (0,)), ((), ()))

    def one_head(head_item):
        query_h, grad_h, delta_h, head_slot = head_item
        key_h = lax.dynamic_index_in_dim(
            key_heads, head_slot // query_group_width, 0, keepdims=False
        )
        value_h = lax.dynamic_index_in_dim(
            value_heads, head_slot // query_group_width, 0, keepdims=False
        )
        scores = (
            lax.dot_general(query_h, key_h, contract_last, preferred_element_type=jnp.float32)
            * score_scaling
        )
        scores = jnp.where(allowed, scores, -jnp.inf)
        peak = jnp.max(scores, axis=1, keepdims=True)
        lse = peak + jnp.log(jnp.sum(jnp.exp(scores - peak), axis=1, keepdims=True))
        probs = jnp.exp(scores - lse)
        probability_block = probs.astype(jnp.bfloat16)
        dprobs = lax.dot_general(grad_h, value_h, contract_last, preferred_element_type=jnp.float32)
        score_gradient_block = (probs * (dprobs - delta_h[:, None])).astype(jnp.bfloat16)
        grad_q = (
            jnp.dot(score_gradient_block, key_h, preferred_element_type=jnp.float32) * score_scaling
        ).astype(jnp.bfloat16)
        key_gradient_terms = (
            lax.dot_general(
                score_gradient_block, query_h, contract_first, preferred_element_type=jnp.float32
            )
            * score_scaling
        )
        value_gradient_terms = lax.dot_general(
            probability_block, grad_h, contract_first, preferred_element_type=jnp.float32
        )
        return (grad_q, key_gradient_terms, value_gradient_terms)

    head_slots = jnp.arange(head_count, dtype=jnp.int32)
    grad_q_all, key_terms_all, value_terms_all = lax.map(
        one_head, (query_heads, grad_heads, row_delta.T, head_slots)
    )
    grad_queries = grad_q_all.transpose(1, 0, 2).reshape(row_count, head_count * HEAD_SIZE)
    key_sum = (
        key_terms_all.reshape(kv_count, query_group_width, key_extent, HEAD_SIZE)
        .sum(axis=1)
        .transpose(1, 0, 2)
        .reshape(key_extent, kv_count * HEAD_SIZE)
    )
    value_sum = (
        value_terms_all.reshape(kv_count, query_group_width, key_extent, HEAD_SIZE)
        .sum(axis=1)
        .transpose(1, 0, 2)
        .reshape(key_extent, kv_count * HEAD_SIZE)
    )
    key_pieces = [
        key_sum[part_index * row_count : (part_index + 1) * row_count]
        for part_index in range(reach_devs + 1)
    ]
    value_pieces = [
        value_sum[part_index * row_count : (part_index + 1) * row_count]
        for part_index in range(reach_devs + 1)
    ]
    running = (key_pieces[reach_devs], value_pieces[reach_devs])
    for part_index in range(reach_devs):
        shifted = passed_along(
            (key_pieces[part_index], value_pieces[part_index]), "ctx", part_index - reach_devs
        )
        running = (running[0] + shifted[0], running[1] + shifted[1])
    return (grad_queries, running[0].astype(jnp.bfloat16), running[1].astype(jnp.bfloat16))


def solution(mesh):
    placed = (
        P(("ctx", "head"), None),
        P(("ctx", "head"), None),
        P(("ctx", "head"), None),
        P(("ctx", "head"), None),
        P(("ctx", "head"), None),
        P("ctx", None),
    )
    return jax.shard_map(
        on_device,
        mesh=mesh,
        in_specs=placed,
        out_specs=(P("ctx", "head"), P("ctx", "head"), P("ctx", "head")),
        check_vma=False,
    )
```

profile of v0, /device:TPU:24, one launch (start us, length us, event | category | flops | bytes accessed | tf_op | source)
XLA Modules:
  0.0 216.0 jit_solution(4553552111754635425)
XLA Ops:
  2.1 4.3 %all-to-all-start.1 = ((bf16[32,8,128]{2,0,1:T(8,128)(2,1)}), bf16[32,8,128]{2,0,1:T(8,128)(2,1)S(1)}, u32[]{:S(2)}, u32[]{:S(2)}) async-start(bf16[32,8,128]{2,0,1:T(8,128)(2,1)} %copy_bitcast_fusion.4), calls=%async_computation.1 | async-start | bytes 131072 | tf_op jit(solution)/shard_map/all_to_all | solution.py:20
  8.7 3.4 %all-to-all-done.1 = bf16[32,8,128]{2,0,1:T(8,128)(2,1)S(1)} async-done(((bf16[32,8,128]{2,0,1:T(8,128)(2,1)}), bf16[32,8,128]{2,0,1:T(8,128)(2,1)S(1)}, u32[]{:S(2)}, u32[]{:S(2)}) %all-to-all-start.1) | async-done | bytes 65568 | tf_op jit(solution)/shard_map/all_to_all | solution.py:20
  12.0 3.4 %all-to-all-start.3 = ((bf16[32,8,128]{2,0,1:T(8,128)(2,1)}), bf16[32,8,128]{2,0,1:T(8,128)(2,1)S(1)}, u32[]{:S(2)}, u32[]{:S(2)}) async-start(bf16[32,8,128]{2,0,1:T(8,128)(2,1)} %copy_bitcast_fusion.3), calls=%async_computation.3 | async-start | bytes 131072 | tf_op jit(solution)/shard_map/all_to_all | solution.py:21
  15.4 9.1 %collective-permute-start = (bf16[256,128]{1,0:T(8,128)(2,1)S(1)}, bf16[256,128]{1,0:T(8,128)(2,1)S(1)}, u32[]{:S(2)}, u32[]{:S(2)}) collective-permute-start(bf16[256,128]{1,0:T(8,128)(2,1)S(1)} %bitcast.163), channel_id=1, source_target_pairs={{0,32},{8,40},{16,48},{24,56},{32,64},{40,72},{48,80},{56,88},{64,... | collective-permute-start | bytes 196616 | tf_op jit(solution)/shard_map/ppermute | solution.py:14
  28.0 4.7 %all-to-all-start = ((bf16[32,8,768]{2,0,1:T(8,128)(2,1)}), bf16[32,8,768]{2,0,1:T(8,128)(2,1)S(1)}, u32[]{:S(2)}, u32[]{:S(2)}) async-start(bf16[32,8,768]{2,0,1:T(8,128)(2,1)} %bitcast.117), calls=%async_computation | async-start | bytes 786432 | tf_op jit(solution)/shard_map/all_to_all | solution.py:19
  32.7 3.8 %collective-permute-start.7 = (bf16[256,128]{1,0:T(8,128)(2,1)S(1)}, bf16[256,128]{1,0:T(8,128)(2,1)S(1)}, u32[]{:S(2)}, u32[]{:S(2)}) collective-permute-start(bf16[256,128]{1,0:T(8,128)(2,1)S(1)} %bitcast.158), channel_id=1, source_target_pairs={{0,8},{8,16},{16,24},{24,32},{32,40},{40,48},{48,56},{56,64},{64,7... | collective-permute-start | bytes 196616 | tf_op jit(solution)/shard_map/ppermute | solution.py:14
  36.6 5.2 %collective-permute-start.6 = (bf16[256,128]{1,0:T(8,128)(2,1)S(1)}, bf16[256,128]{1,0:T(8,128)(2,1)S(1)}, u32[]{:S(2)}, u32[]{:S(2)}) collective-permute-start(bf16[256,128]{1,0:T(8,128)(2,1)S(1)} %bitcast.159), channel_id=1, source_target_pairs={{0,16},{8,24},{16,32},{24,40},{32,48},{40,56},{48,64},{56,72},{64,... | collective-permute-start | bytes 196616 | tf_op jit(solution)/shard_map/ppermute | solution.py:14
  41.7 7.7 %collective-permute-start.5 = (bf16[256,128]{1,0:T(8,128)(2,1)S(1)}, bf16[256,128]{1,0:T(8,128)(2,1)S(1)}, u32[]{:S(2)}, u32[]{:S(2)}) collective-permute-start(bf16[256,128]{1,0:T(8,128)(2,1)S(1)} %bitcast.160), channel_id=1, source_target_pairs={{0,24},{8,32},{16,40},{24,48},{32,56},{40,64},{48,72},{56,80},{64,... | collective-permute-start | bytes 196616 | tf_op jit(solution)/shard_map/ppermute | solution.py:14
  49.5 9.1 %collective-permute-start.4 = (bf16[256,128]{1,0:T(8,128)(2,1)S(1)}, bf16[256,128]{1,0:T(8,128)(2,1)S(1)}, u32[]{:S(2)}, u32[]{:S(2)}) collective-permute-start(bf16[256,128]{1,0:T(8,128)(2,1)S(1)} %bitcast.161), channel_id=1, source_target_pairs={{0,32},{8,40},{16,48},{24,56},{32,64},{40,72},{48,80},{56,88},{64,... | collective-permute-start | bytes 196616 | tf_op jit(solution)/shard_map/ppermute | solution.py:14
  58.6 6.8 %collective-permute-start.1 = (bf16[256,128]{1,0:T(8,128)(2,1)S(1)}, bf16[256,128]{1,0:T(8,128)(2,1)S(1)}, u32[]{:S(2)}, u32[]{:S(2)}) collective-permute-start(bf16[256,128]{1,0:T(8,128)(2,1)S(1)} %bitcast.164), channel_id=1, source_target_pairs={{0,24},{8,32},{16,40},{24,48},{32,56},{40,64},{48,72},{56,80},{64,... | collective-permute-start | bytes 196616 | tf_op jit(solution)/shard_map/ppermute | solution.py:14
  65.5 5.0 %collective-permute-done.1 = bf16[256,128]{1,0:T(8,128)(2,1)S(1)} collective-permute-done((bf16[256,128]{1,0:T(8,128)(2,1)S(1)}, bf16[256,128]{1,0:T(8,128)(2,1)S(1)}, u32[]{:S(2)}, u32[]{:S(2)}) %collective-permute-start.1) | collective-permute-done | bytes 65568 | tf_op jit(solution)/shard_map/ppermute | solution.py:14
  70.5 5.3 %collective-permute-start.2 = (bf16[256,128]{1,0:T(8,128)(2,1)S(1)}, bf16[256,128]{1,0:T(8,128)(2,1)S(1)}, u32[]{:S(2)}, u32[]{:S(2)}) collective-permute-start(bf16[256,128]{1,0:T(8,128)(2,1)S(1)} %bitcast.165), channel_id=1, source_target_pairs={{0,16},{8,24},{16,32},{24,40},{32,48},{40,56},{48,64},{56,72},{64,... | collective-permute-start | bytes 196616 | tf_op jit(solution)/shard_map/ppermute | solution.py:14
  75.8 3.9 %collective-permute-done.2 = bf16[256,128]{1,0:T(8,128)(2,1)S(1)} collective-permute-done((bf16[256,128]{1,0:T(8,128)(2,1)S(1)}, bf16[256,128]{1,0:T(8,128)(2,1)S(1)}, u32[]{:S(2)}, u32[]{:S(2)}) %collective-permute-start.2) | collective-permute-done | bytes 65568 | tf_op jit(solution)/shard_map/ppermute | solution.py:14
  79.7 4.0 %collective-permute-start.3 = (bf16[256,128]{1,0:T(8,128)(2,1)S(1)}, bf16[256,128]{1,0:T(8,128)(2,1)S(1)}, u32[]{:S(2)}, u32[]{:S(2)}) collective-permute-start(bf16[256,128]{1,0:T(8,128)(2,1)S(1)} %bitcast.166), channel_id=1, source_target_pairs={{0,8},{8,16},{16,24},{24,32},{32,40},{40,48},{48,56},{56,64},{64,7... | collective-permute-start | bytes 196616 | tf_op jit(solution)/shard_map/ppermute | solution.py:14
  83.7 4.2 %collective-permute-done.3 = bf16[256,128]{1,0:T(8,128)(2,1)S(1)} collective-permute-done((bf16[256,128]{1,0:T(8,128)(2,1)S(1)}, bf16[256,128]{1,0:T(8,128)(2,1)S(1)}, u32[]{:S(2)}, u32[]{:S(2)}) %collective-permute-start.3) | collective-permute-done | bytes 65568 | tf_op jit(solution)/shard_map/ppermute | solution.py:14
  88.0 3.9 %all-to-all-start.4 = ((bf16[32,8,768]{2,0,1:T(8,128)(2,1)}), bf16[32,8,768]{2,0,1:T(8,128)(2,1)S(1)}, u32[]{:S(2)}, u32[]{:S(2)}) async-start(bf16[32,8,768]{2,0,1:T(8,128)(2,1)} %bitcast.115), calls=%async_computation.4 | async-start | bytes 786432 | tf_op jit(solution)/shard_map/all_to_all | solution.py:22
  91.9 8.8 %all-to-all-done.4 = bf16[32,8,768]{2,0,1:T(8,128)(2,1)S(1)} async-done(((bf16[32,8,768]{2,0,1:T(8,128)(2,1)}), bf16[32,8,768]{2,0,1:T(8,128)(2,1)S(1)}, u32[]{:S(2)}, u32[]{:S(2)}) %all-to-all-start.4) | async-done | bytes 393248 | tf_op jit(solution)/shard_map/all_to_all | solution.py:22
  100.7 4.1 %all-to-all-start.2 = ((bf16[32,8,768]{2,0,1:T(8,128)(2,1)}), bf16[32,8,768]{2,0,1:T(8,128)(2,1)}, u32[]{:S(2)}, u32[]{:S(2)}) async-start(bf16[32,8,768]{2,0,1:T(8,128)(2,1)} %bitcast.116), calls=%async_computation.2 | async-start | bytes 786432 | tf_op jit(solution)/shard_map/all_to_all | solution.py:23
  105.6 8.2 %all-to-all-done.2 = bf16[32,8,768]{2,0,1:T(8,128)(2,1)} async-done(((bf16[32,8,768]{2,0,1:T(8,128)(2,1)}), bf16[32,8,768]{2,0,1:T(8,128)(2,1)}, u32[]{:S(2)}, u32[]{:S(2)}) %all-to-all-start.2) | async-done | bytes 393248 | tf_op jit(solution)/shard_map/all_to_all | solution.py:23
  115.7 34.4 %while.16 = (s32[]{:T(128)}, bf16[6,256,128]{1,2,0:T(8,128)(2,1)}, f32[6,1280,128]{2,1,0:T(8,128)}, f32[6,1280,128]{2,1,0:T(8,128)}, bf16[6,256,128]{2,1,0:T(8,1...) while((s32[]{:T(128)}, bf16[6,256,128]{1,2,0:T(8,128)(2,1)}, ...), condition=%wide.region_5.6_spmd.clone, body=%wide.region_2.5_spmd.clone.sunk | while | flops 423264000 | bytes 13253821 | solution.py:92
  129.5 2.3 %fusion.73 = f32[6,1280,128]{2,1,0:T(8,128)} fusion(f32[6,1280,128]{2,1,0:T(8,128)} %get-tuple-element.255, s32[]{:T(128)S(6)} %copy.73, f32[256,1280]{1,0:T(8,128)S(1)} %get-tuple-element.239, f32[256]{0:T(256)S(1)} %log_add_fusion.2, bf16[6,256,128]{2,1,0:T(8,128)(2,1)} %copy-done.1), kind=kOutput, calls=%fused_computation.10.clone.1 | convolution fusion | flops 84541440 | bytes 2033664 | tf_op jit(solution)/shard_map/while/body/eval_jaxpr/dot_general | solution.py:86
  150.1 2.4 %reduce_sum.44 = f32[1280,128]{1,0:T(8,128)S(1)} reduce(f32[6,1280,128]{2,1,0:T(8,128)} %get-tuple-element.83, f32[]{:T(128)} %constant.67.clone.1), dimensions={0}, to_apply=%region_7.8 | reduce | flops 819200 | bytes 4587524 | tf_op jit(solution)/shard_map/reduce_sum | solution.py:104
  152.5 2.4 %reduce_sum.42 = f32[1280,128]{1,0:T(8,128)S(1)} reduce(f32[6,1280,128]{2,1,0:T(8,128)} %get-tuple-element.82, f32[]{:T(128)} %constant.67.clone.1), dimensions={0}, to_apply=%region_6.7 | reduce | flops 819200 | bytes 4587524 | tf_op jit(solution)/shard_map/reduce_sum | solution.py:98
  159.9 6.7 %collective-permute-start.14 = (f32[256,128]{1,0:T(8,128)S(1)}, f32[256,128]{1,0:T(8,128)S(1)}, u32[]{:S(2)}, u32[]{:S(2)}) collective-permute-start(f32[256,128]{1,0:T(8,128)S(1)} %get-tuple-element.170), channel_id=1, source_target_pairs={{16,0},{24,8},{32,16},{40,24},{48,32},{56,40},{64,48},{72,56},{80,... | collective-permute-start | bytes 393224 | tf_op jit(solution)/shard_map/ppermute | solution.py:14
  166.7 3.5 %collective-permute-start.13 = (f32[256,128]{1,0:T(8,128)S(1)}, f32[256,128]{1,0:T(8,128)S(1)}, u32[]{:S(2)}, u32[]{:S(2)}) collective-permute-start(f32[256,128]{1,0:T(8,128)S(1)} %get-tuple-element.171), channel_id=1, source_target_pairs={{24,0},{32,8},{40,16},{48,24},{56,32},{64,40},{72,48},{80,56},{88,... | collective-permute-start | bytes 393224 | tf_op jit(solution)/shard_map/ppermute | solution.py:14
  170.2 6.6 %collective-permute-start.8 = (f32[256,128]{1,0:T(8,128)S(1)}, f32[256,128]{1,0:T(8,128)S(1)}, u32[]{:S(2)}, u32[]{:S(2)}) collective-permute-start(f32[256,128]{1,0:T(8,128)S(1)} %get-tuple-element.172), channel_id=1, source_target_pairs={{32,0},{40,8},{48,16},{56,24},{64,32},{72,40},{80,48},{88,56},{96,... | collective-permute-start | bytes 393224 | tf_op jit(solution)/shard_map/ppermute | solution.py:14
  176.9 3.9 %collective-permute-start.11 = (f32[256,128]{1,0:T(8,128)S(1)}, f32[256,128]{1,0:T(8,128)S(1)}, u32[]{:S(2)}, u32[]{:S(2)}) collective-permute-start(f32[256,128]{1,0:T(8,128)S(1)} %get-tuple-element.173), channel_id=1, source_target_pairs={{8,0},{16,8},{24,16},{32,24},{40,32},{48,40},{56,48},{64,56},{72,6... | collective-permute-start | bytes 393224 | tf_op jit(solution)/shard_map/ppermute | solution.py:14
  180.8 3.0 %collective-permute-start.10 = (f32[256,128]{1,0:T(8,128)S(1)}, f32[256,128]{1,0:T(8,128)S(1)}, u32[]{:S(2)}, u32[]{:S(2)}) collective-permute-start(f32[256,128]{1,0:T(8,128)S(1)} %get-tuple-element.174), channel_id=1, source_target_pairs={{16,0},{24,8},{32,16},{40,24},{48,32},{56,40},{64,48},{72,56},{80,... | collective-permute-start | bytes 393224 | tf_op jit(solution)/shard_map/ppermute | solution.py:14
  183.8 4.5 %collective-permute-start.9 = (f32[256,128]{1,0:T(8,128)S(1)}, f32[256,128]{1,0:T(8,128)S(1)}, u32[]{:S(2)}, u32[]{:S(2)}) collective-permute-start(f32[256,128]{1,0:T(8,128)S(1)} %get-tuple-element.175), channel_id=1, source_target_pairs={{24,0},{32,8},{40,16},{48,24},{56,32},{64,40},{72,48},{80,56},{88,... | collective-permute-start | bytes 393224 | tf_op jit(solution)/shard_map/ppermute | solution.py:14
  189.2 12.8 %collective-permute-done.8 = f32[256,128]{1,0:T(8,128)S(1)} collective-permute-done((f32[256,128]{1,0:T(8,128)S(1)}, f32[256,128]{1,0:T(8,128)S(1)}, u32[]{:S(2)}, u32[]{:S(2)}) %collective-permute-start.8) | collective-permute-done | bytes 131104 | tf_op jit(solution)/shard_map/ppermute | solution.py:14
  202.0 3.2 %collective-permute-done.10 = f32[256,128]{1,0:T(8,128)S(1)} collective-permute-done((f32[256,128]{1,0:T(8,128)S(1)}, f32[256,128]{1,0:T(8,128)S(1)}, u32[]{:S(2)}, u32[]{:S(2)}) %collective-permute-start.10) | collective-permute-done | bytes 131104 | tf_op jit(solution)/shard_map/ppermute | solution.py:14
  205.2 10.0 %collective-permute-done.9 = f32[256,128]{1,0:T(8,128)S(1)} collective-permute-done((f32[256,128]{1,0:T(8,128)S(1)}, f32[256,128]{1,0:T(8,128)S(1)}, u32[]{:S(2)}, u32[]{:S(2)}) %collective-permute-start.9) | collective-permute-done | bytes 131104 | tf_op jit(solution)/shard_map/ppermute | solution.py:14
  (139 shorter events, 48.5 us)
Async XLA Ops:
  0.6 0.8 copy-start
  0.6 25.7 %copy-start.3 = (bf16[32,6144]{1,0:T(8,128)(2,1)S(1)}, bf16[32,6144]{1,0:T(8,128)(2,1)}, u32[]{:S(2)}) copy-start(bf16[32,6144]{1,0:T(8,128)(2,1)} %param.11) | copy-start | bytes 1179652
  1.5 25.7 %copy-start.4 = (bf16[32,6144]{1,0:T(8,128)(2,1)S(1)}, bf16[32,6144]{1,0:T(8,128)(2,1)}, u32[]{:S(2)}) copy-start(bf16[32,6144]{1,0:T(8,128)(2,1)} %param.12) | copy-start | bytes 1179652
  2.1 9.9 %all-to-all-start.1 = ((bf16[32,8,128]{2,0,1:T(8,128)(2,1)}), bf16[32,8,128]{2,0,1:T(8,128)(2,1)S(1)}, u32[]{:S(2)}, u32[]{:S(2)}) async-start(bf16[32,8,128]{2,0,1:T(8,128)(2,1)} %copy_bitcast_fusion.4), calls=%async_computation.1 | async-start | bytes 131072 | tf_op jit(solution)/shard_map/all_to_all | solution.py:20
  12.0 16.0 %all-to-all-start.3 = ((bf16[32,8,128]{2,0,1:T(8,128)(2,1)}), bf16[32,8,128]{2,0,1:T(8,128)(2,1)S(1)}, u32[]{:S(2)}, u32[]{:S(2)}) async-start(bf16[32,8,128]{2,0,1:T(8,128)(2,1)} %copy_bitcast_fusion.3), calls=%async_computation.3 | async-start | bytes 131072 | tf_op jit(solution)/shard_map/all_to_all | solution.py:21
  15.4 43.2 %collective-permute-start = (bf16[256,128]{1,0:T(8,128)(2,1)S(1)}, bf16[256,128]{1,0:T(8,128)(2,1)S(1)}, u32[]{:S(2)}, u32[]{:S(2)}) collective-permute-start(bf16[256,128]{1,0:T(8,128)(2,1)S(1)} %bitcast.163), channel_id=1, source_target_pairs={{0,32},{8,40},{16,48},{24,56},{32,64},{40,72},{48,80},{56,88},{64,... | collective-permute-start | bytes 196616 | tf_op jit(solution)/shard_map/ppermute | solution.py:14
  28.0 59.9 %all-to-all-start = ((bf16[32,8,768]{2,0,1:T(8,128)(2,1)}), bf16[32,8,768]{2,0,1:T(8,128)(2,1)S(1)}, u32[]{:S(2)}, u32[]{:S(2)}) async-start(bf16[32,8,768]{2,0,1:T(8,128)(2,1)} %bitcast.117), calls=%async_computation | async-start | bytes 786432 | tf_op jit(solution)/shard_map/all_to_all | solution.py:19
  32.7 59.2 %collective-permute-start.7 = (bf16[256,128]{1,0:T(8,128)(2,1)S(1)}, bf16[256,128]{1,0:T(8,128)(2,1)S(1)}, u32[]{:S(2)}, u32[]{:S(2)}) collective-permute-start(bf16[256,128]{1,0:T(8,128)(2,1)S(1)} %bitcast.158), channel_id=1, source_target_pairs={{0,8},{8,16},{16,24},{24,32},{32,40},{40,48},{48,56},{56,64},{64,7... | collective-permute-start | bytes 196616 | tf_op jit(solution)/shard_map/ppermute | solution.py:14
  36.6 55.3 %collective-permute-start.6 = (bf16[256,128]{1,0:T(8,128)(2,1)S(1)}, bf16[256,128]{1,0:T(8,128)(2,1)S(1)}, u32[]{:S(2)}, u32[]{:S(2)}) collective-permute-start(bf16[256,128]{1,0:T(8,128)(2,1)S(1)} %bitcast.159), channel_id=1, source_target_pairs={{0,16},{8,24},{16,32},{24,40},{32,48},{40,56},{48,64},{56,72},{64,... | collective-permute-start | bytes 196616 | tf_op jit(solution)/shard_map/ppermute | solution.py:14
  41.7 50.1 %collective-permute-start.5 = (bf16[256,128]{1,0:T(8,128)(2,1)S(1)}, bf16[256,128]{1,0:T(8,128)(2,1)S(1)}, u32[]{:S(2)}, u32[]{:S(2)}) collective-permute-start(bf16[256,128]{1,0:T(8,128)(2,1)S(1)} %bitcast.160), channel_id=1, source_target_pairs={{0,24},{8,32},{16,40},{24,48},{32,56},{40,64},{48,72},{56,80},{64,... | collective-permute-start | bytes 196616 | tf_op jit(solution)/shard_map/ppermute | solution.py:14
  49.5 42.3 %collective-permute-start.4 = (bf16[256,128]{1,0:T(8,128)(2,1)S(1)}, bf16[256,128]{1,0:T(8,128)(2,1)S(1)}, u32[]{:S(2)}, u32[]{:S(2)}) collective-permute-start(bf16[256,128]{1,0:T(8,128)(2,1)S(1)} %bitcast.161), channel_id=1, source_target_pairs={{0,32},{8,40},{16,48},{24,56},{32,64},{40,72},{48,80},{56,88},{64,... | collective-permute-start | bytes 196616 | tf_op jit(solution)/shard_map/ppermute | solution.py:14
  58.6 11.8 %collective-permute-start.1 = (bf16[256,128]{1,0:T(8,128)(2,1)S(1)}, bf16[256,128]{1,0:T(8,128)(2,1)S(1)}, u32[]{:S(2)}, u32[]{:S(2)}) collective-permute-start(bf16[256,128]{1,0:T(8,128)(2,1)S(1)} %bitcast.164), channel_id=1, source_target_pairs={{0,24},{8,32},{16,40},{24,48},{32,56},{40,64},{48,72},{56,80},{64,... | collective-permute-start | bytes 196616 | tf_op jit(solution)/shard_map/ppermute | solution.py:14
  70.5 9.2 %collective-permute-start.2 = (bf16[256,128]{1,0:T(8,128)(2,1)S(1)}, bf16[256,128]{1,0:T(8,128)(2,1)S(1)}, u32[]{:S(2)}, u32[]{:S(2)}) collective-permute-start(bf16[256,128]{1,0:T(8,128)(2,1)S(1)} %bitcast.165), channel_id=1, source_target_pairs={{0,16},{8,24},{16,32},{24,40},{32,48},{40,56},{48,64},{56,72},{64,... | collective-permute-start | bytes 196616 | tf_op jit(solution)/shard_map/ppermute | solution.py:14
  79.7 8.3 %collective-permute-start.3 = (bf16[256,128]{1,0:T(8,128)(2,1)S(1)}, bf16[256,128]{1,0:T(8,128)(2,1)S(1)}, u32[]{:S(2)}, u32[]{:S(2)}) collective-permute-start(bf16[256,128]{1,0:T(8,128)(2,1)S(1)} %bitcast.166), channel_id=1, source_target_pairs={{0,8},{8,16},{16,24},{24,32},{32,40},{40,48},{48,56},{56,64},{64,7... | collective-permute-start | bytes 196616 | tf_op jit(solution)/shard_map/ppermute | solution.py:14
  88.0 12.8 %all-to-all-start.4 = ((bf16[32,8,768]{2,0,1:T(8,128)(2,1)}), bf16[32,8,768]{2,0,1:T(8,128)(2,1)S(1)}, u32[]{:S(2)}, u32[]{:S(2)}) async-start(bf16[32,8,768]{2,0,1:T(8,128)(2,1)} %bitcast.115), calls=%async_computation.4 | async-start | bytes 786432 | tf_op jit(solution)/shard_map/all_to_all | solution.py:22
  100.7 13.0 %all-to-all-start.2 = ((bf16[32,8,768]{2,0,1:T(8,128)(2,1)}), bf16[32,8,768]{2,0,1:T(8,128)(2,1)}, u32[]{:S(2)}, u32[]{:S(2)}) async-start(bf16[32,8,768]{2,0,1:T(8,128)(2,1)} %bitcast.116), calls=%async_computation.2 | async-start | bytes 786432 | tf_op jit(solution)/shard_map/all_to_all | solution.py:23
  115.7 0.8 copy-start.1
  118.0 3.4 %copy-start.2 = (bf16[6,256,128]{2,1,0:T(8,128)(2,1)S(1)}, bf16[6,256,128]{2,1,0:T(8,128)(2,1)}, u32[]{:S(2)}) copy-start(bf16[6,256,128]{2,1,0:T(8,128)(2,1)} %copy-done.1) | copy-start | bytes 1179652 | tf_op jit(solution)/shard_map/while
  123.7 3.5 %copy-start.2 = (bf16[6,256,128]{2,1,0:T(8,128)(2,1)S(1)}, bf16[6,256,128]{2,1,0:T(8,128)(2,1)}, u32[]{:S(2)}) copy-start(bf16[6,256,128]{2,1,0:T(8,128)(2,1)} %copy-done.1) | copy-start | bytes 1179652 | tf_op jit(solution)/shard_map/while
  129.5 3.5 %copy-start.2 = (bf16[6,256,128]{2,1,0:T(8,128)(2,1)S(1)}, bf16[6,256,128]{2,1,0:T(8,128)(2,1)}, u32[]{:S(2)}) copy-start(bf16[6,256,128]{2,1,0:T(8,128)(2,1)} %copy-done.1) | copy-start | bytes 1179652 | tf_op jit(solution)/shard_map/while
  135.2 3.5 %copy-start.2 = (bf16[6,256,128]{2,1,0:T(8,128)(2,1)S(1)}, bf16[6,256,128]{2,1,0:T(8,128)(2,1)}, u32[]{:S(2)}) copy-start(bf16[6,256,128]{2,1,0:T(8,128)(2,1)} %copy-done.1) | copy-start | bytes 1179652 | tf_op jit(solution)/shard_map/while
  140.9 3.5 %copy-start.2 = (bf16[6,256,128]{2,1,0:T(8,128)(2,1)S(1)}, bf16[6,256,128]{2,1,0:T(8,128)(2,1)}, u32[]{:S(2)}) copy-start(bf16[6,256,128]{2,1,0:T(8,128)(2,1)} %copy-done.1) | copy-start | bytes 1179652 | tf_op jit(solution)/shard_map/while
  146.7 3.5 %copy-start.2 = (bf16[6,256,128]{2,1,0:T(8,128)(2,1)S(1)}, bf16[6,256,128]{2,1,0:T(8,128)(2,1)}, u32[]{:S(2)}) copy-start(bf16[6,256,128]{2,1,0:T(8,128)(2,1)} %copy-done.1) | copy-start | bytes 1179652 | tf_op jit(solution)/shard_map/while
  152.5 2.4 %copy-start.5 = (bf16[6,256,128]{1,2,0:T(8,128)(2,1)S(1)}, bf16[6,256,128]{1,2,0:T(8,128)(2,1)}, u32[]{:S(2)}) copy-start(bf16[6,256,128]{1,2,0:T(8,128)(2,1)} %get-tuple-element.81) | copy-start | bytes 1179652
  155.9 20.9 %collective-permute-start.12 = (f32[256,128]{1,0:T(8,128)S(1)}, f32[256,128]{1,0:T(8,128)S(1)}, u32[]{:S(2)}, u32[]{:S(2)}) collective-permute-start(f32[256,128]{1,0:T(8,128)S(1)} %get-tuple-element.168), channel_id=1, source_target_pairs={{32,0},{40,8},{48,16},{56,24},{64,32},{72,40},{80,48},{88,56},{96,... | collective-permute-start | bytes 393224 | tf_op jit(solution)/shard_map/ppermute | solution.py:14
  157.8 22.9 %collective-permute-start.15 = (f32[256,128]{1,0:T(8,128)S(1)}, f32[256,128]{1,0:T(8,128)S(1)}, u32[]{:S(2)}, u32[]{:S(2)}) collective-permute-start(f32[256,128]{1,0:T(8,128)S(1)} %get-tuple-element.169), channel_id=1, source_target_pairs={{8,0},{16,8},{24,16},{32,24},{40,32},{48,40},{56,48},{64,56},{72,6... | collective-permute-start | bytes 393224 | tf_op jit(solution)/shard_map/ppermute | solution.py:14
  159.9 23.9 %collective-permute-start.14 = (f32[256,128]{1,0:T(8,128)S(1)}, f32[256,128]{1,0:T(8,128)S(1)}, u32[]{:S(2)}, u32[]{:S(2)}) collective-permute-start(f32[256,128]{1,0:T(8,128)S(1)} %get-tuple-element.170), channel_id=1, source_target_pairs={{16,0},{24,8},{32,16},{40,24},{48,32},{56,40},{64,48},{72,56},{80,... | collective-permute-start | bytes 393224 | tf_op jit(solution)/shard_map/ppermute | solution.py:14
  166.7 21.9 %collective-permute-start.13 = (f32[256,128]{1,0:T(8,128)S(1)}, f32[256,128]{1,0:T(8,128)S(1)}, u32[]{:S(2)}, u32[]{:S(2)}) collective-permute-start(f32[256,128]{1,0:T(8,128)S(1)} %get-tuple-element.171), channel_id=1, source_target_pairs={{24,0},{32,8},{40,16},{48,24},{56,32},{64,40},{72,48},{80,56},{88,... | collective-permute-start | bytes 393224 | tf_op jit(solution)/shard_map/ppermute | solution.py:14
  170.2 31.8 %collective-permute-start.8 = (f32[256,128]{1,0:T(8,128)S(1)}, f32[256,128]{1,0:T(8,128)S(1)}, u32[]{:S(2)}, u32[]{:S(2)}) collective-permute-start(f32[256,128]{1,0:T(8,128)S(1)} %get-tuple-element.172), channel_id=1, source_target_pairs={{32,0},{40,8},{48,16},{56,24},{64,32},{72,40},{80,48},{88,56},{96,... | collective-permute-start | bytes 393224 | tf_op jit(solution)/shard_map/ppermute | solution.py:14
  176.9 25.1 %collective-permute-start.11 = (f32[256,128]{1,0:T(8,128)S(1)}, f32[256,128]{1,0:T(8,128)S(1)}, u32[]{:S(2)}, u32[]{:S(2)}) collective-permute-start(f32[256,128]{1,0:T(8,128)S(1)} %get-tuple-element.173), channel_id=1, source_target_pairs={{8,0},{16,8},{24,16},{32,24},{40,32},{48,40},{56,48},{64,56},{72,6... | collective-permute-start | bytes 393224 | tf_op jit(solution)/shard_map/ppermute | solution.py:14
  180.8 24.5 %collective-permute-start.10 = (f32[256,128]{1,0:T(8,128)S(1)}, f32[256,128]{1,0:T(8,128)S(1)}, u32[]{:S(2)}, u32[]{:S(2)}) collective-permute-start(f32[256,128]{1,0:T(8,128)S(1)} %get-tuple-element.174), channel_id=1, source_target_pairs={{16,0},{24,8},{32,16},{40,24},{48,32},{56,40},{64,48},{72,56},{80,... | collective-permute-start | bytes 393224 | tf_op jit(solution)/shard_map/ppermute | solution.py:14
  183.8 31.4 %collective-permute-start.9 = (f32[256,128]{1,0:T(8,128)S(1)}, f32[256,128]{1,0:T(8,128)S(1)}, u32[]{:S(2)}, u32[]{:S(2)}) collective-permute-start(f32[256,128]{1,0:T(8,128)S(1)} %get-tuple-element.175), channel_id=1, source_target_pairs={{24,0},{32,8},{40,16},{48,24},{56,32},{64,40},{72,48},{80,56},{88,... | collective-permute-start | bytes 393224 | tf_op jit(solution)/shard_map/ppermute | solution.py:14
  (5 other events, 4.0 us)
where the time goes:
time: 220 us; the launch traced here: 216 us
  starting transfers between devices  104 us (47%)
  waiting for transfers between devices  59.8 us (27%)
  matrix products  27.4 us (12%)
  local copies, waits for them, and re-layouts  14.4 us (7%)
  other arithmetic  9.48 us (4%)
    ppermute x16, starting transfers between devices, passed_along(): lax.ppermute(value, axis, [(source, source + steps) for source in range(i...  83.3 us
    ppermute x16, waiting for transfers between devices, passed_along(): lax.ppermute(value, axis, [(source, source + steps) for source in range(i...  39.4 us
    dot_general x6, matrix products, one_head(): lax.dot_general(probability_block, grad_h, contract_first, preferred_elem...  13.4 us
    all_to_all x1, waiting for transfers between devices, on_device(): lax.all_to_all(outputs, 'head', split_axis=1, concat_axis=0, tiled=True)  8.8 us
    all_to_all x1, waiting for transfers between devices, on_device(): lax.all_to_all(out_grad, 'head', split_axis=1, concat_axis=0, tiled=True)  8.18 us
    dot_general x6, matrix products, one_head(): lax.dot_general(score_gradient_block, query_h, contract_first, preferred_...  7.38 us
    all_to_all x1, starting transfers between devices, on_device(): lax.all_to_all(queries, 'head', split_axis=1, concat_axis=0, tiled=True)  4.71 us
    dynamic_update_slice x12, local copies, waits for them, and re-layouts, on_device(): lax.map(one_head, (query_heads, grad_heads, row_delta.T, head_slots))  4.48 us
  transfers between devices with their start and end apart: 21, of which 10 were waited for; matrix products, arithmetic and copies ran while one was open for 3% of the time, Pallas kernels for 0%

commit v1 on v0

v1 whole, which is shorter than its diff:
```python
import functools

import jax
import jax.numpy as jnp
from jax import lax
from jax.experimental import pallas as pl
from jax.experimental.pallas import tpu as pltpu
from jax.sharding import PartitionSpec as P

HEAD = 128
GROUP = 6
KV_HEADS = 8
TOK = 256
ROWS = 32
REACH = 4
SCALE = HEAD ** (-0.5)
QG = 2 * GROUP * HEAD
WIDE = QG + HEAD
F32 = jnp.float32
BF16 = jnp.bfloat16
VMEM = pl.BlockSpec(memory_space=pltpu.VMEM)
SMEM = pl.BlockSpec(memory_space=pltpu.SMEM)


def shifted(value, steps):
    count = lax.axis_size("ctx")
    first, last = max(0, -steps), min(count, count - steps)
    return lax.ppermute(value, "ctx", [(s, s + steps) for s in range(first, last)])


def regroup(value):
    return lax.all_to_all(value, "head", split_axis=0, concat_axis=0, tiled=True)


def pack_kv_kernel(k_ref, v_ref, out_ref):
    for h in range(KV_HEADS):
        out_ref[h, :, :HEAD] = k_ref[:, h * HEAD : (h + 1) * HEAD]
        out_ref[h, :, HEAD:] = v_ref[:, h * HEAD : (h + 1) * HEAD]


def pack_qg_kernel(q_ref, g_ref, o_ref, out_ref):
    lane = lax.broadcasted_iota(jnp.int32, (ROWS, HEAD), 1)
    width = GROUP * HEAD
    for h in range(KV_HEADS):
        out_ref[h, :, :width] = q_ref[:, h * width : (h + 1) * width]
        out_ref[h, :, width:QG] = g_ref[:, h * width : (h + 1) * width]
        delta = jnp.zeros((ROWS, HEAD), F32)
        for i in range(GROUP):
            cols = slice(h * width + i * HEAD, h * width + (i + 1) * HEAD)
            term = jnp.sum(g_ref[:, cols].astype(F32) * o_ref[:, cols].astype(F32), axis=1, keepdims=True)
            delta = jnp.where(jnp.bitwise_and(lane, 7) == i, term, delta)
        high = delta.astype(BF16).astype(F32)
        rest = delta - high
        middle = rest.astype(BF16).astype(F32)
        low = rest - middle
        mixed = jnp.where(lane < 8, high, jnp.where(lane < 16, middle, low))
        out_ref[h, :, QG:] = mixed.astype(BF16)


def dot(a, b, dims):
    return lax.dot_general(a, b, (dims, ((), ())), preferred_element_type=F32)


NT = ((1,), (1,))
NN = ((1,), (0,))


def attention_kernel(
    lists_ref, qg_ref, kv0_ref, kv13_ref, kv2_ref, kv4_ref,
    dq_ref, send_ref, keep_ref, own_ref,
    delta_ref, kt_ref, acc_ref,
):
    def kv(o):
        return {
            0: kv0_ref, 1: kv13_ref.at[:TOK], 2: kv2_ref, 3: kv13_ref.at[TOK:], 4: kv4_ref,
        }[o]

    offsets = range(REACH + 1)
    for o in offsets:
        kt_ref[:, o * TOK : (o + 1) * TOK] = kv(o)[:, :HEAD].T
    packed = qg_ref[:, QG:].astype(F32).T
    delta_ref[...] = packed[0:8] + packed[8:16] + packed[16:24]
    acc_ref[...] = jnp.zeros_like(acc_ref)
    listed = [lists_ref[0, o] >= 0 for o in offsets]

    def head(i, carry):
        q = qg_ref[:, pl.ds(pl.multiple_of(i * HEAD, HEAD), HEAD)]
        g = qg_ref[:, pl.ds(pl.multiple_of((GROUP + i) * HEAD, HEAD), HEAD)]
        delta = delta_ref[pl.ds(i, 1), :]
        scores = [dot(kv(o)[:, :HEAD], q, NT) for o in offsets]
        peak = jnp.full((1, TOK), -jnp.inf, F32)
        for o in offsets:
            top = jnp.max(scores[o], axis=0, keepdims=True)
            peak = jnp.maximum(peak, jnp.where(listed[o], top, -jnp.inf))
        weights, total = [], jnp.zeros((1, TOK), F32)
        for o in offsets:
            bound = jnp.where(listed[o], peak, jnp.inf)
            w = jnp.exp((scores[o] - bound) * SCALE)
            weights.append(w)
            total = total + jnp.sum(w, axis=0, keepdims=True)
        inverse = 1.0 / total
        dqt = jnp.zeros((HEAD, TOK), F32)
        for o in offsets:
            probs = weights[o] * inverse
            dprobs = dot(kv(o)[:, HEAD:], g, NT)
            ds = (probs * (dprobs - delta)).astype(BF16)
            acc_ref[o, :, :HEAD] += dot(ds, q, NN)
            acc_ref[o, :, HEAD:] += dot(probs.astype(BF16), g, NN)
            dqt = dqt + dot(kt_ref[:, o * TOK : (o + 1) * TOK], ds, NN)
        dq_ref[:, pl.ds(pl.multiple_of(i * HEAD, HEAD), HEAD)] = (dqt * SCALE).T.astype(BF16)
        return carry

    lax.fori_loop(0, GROUP, head, 0)
    scale = jnp.where(lax.broadcasted_iota(jnp.int32, (1, 2 * HEAD), 1) < HEAD, SCALE, 1.0)
    send_ref[:TOK] = (acc_ref[4] * scale).astype(BF16)
    send_ref[TOK:] = (acc_ref[2] * scale).astype(BF16)
    keep_ref[:TOK] = acc_ref[3] * scale
    keep_ref[TOK:] = acc_ref[1] * scale
    own_ref[...] = acc_ref[0] * scale


def on_device(queries, keys, values, outputs, out_grad, frame_lists):
    kv_packed = pl.pallas_call(
        pack_kv_kernel,
        out_shape=jax.ShapeDtypeStruct((KV_HEADS, ROWS, 2 * HEAD), BF16),
        in_specs=[VMEM] * 2,
        out_specs=VMEM,
        compiler_params=pltpu.CompilerParams(vmem_limit_bytes=2 << 20),
        name="pack_kv",
    )(keys, values)
    qg_packed = pl.pallas_call(
        pack_qg_kernel,
        out_shape=jax.ShapeDtypeStruct((KV_HEADS, ROWS, WIDE), BF16),
        in_specs=[VMEM] * 3,
        out_specs=VMEM,
        cost_estimate=pl.CostEstimate(flops=1_000_000, bytes_accessed=3_000_000, transcendentals=0),
        compiler_params=pltpu.CompilerParams(vmem_limit_bytes=6 << 20),
        name="pack_qg",
    )(queries, out_grad, outputs)
    kv0 = regroup(kv_packed).reshape(TOK, 2 * HEAD)
    qg = regroup(qg_packed).reshape(TOK, WIDE)
    kv2 = shifted(kv0, 2)
    kv13 = shifted(jnp.concatenate([kv0, kv2], axis=0), 1)
    kv4 = shifted(kv2, 2)
    width = 2 * HEAD
    dq, send, keep, own = pl.pallas_call(
        attention_kernel,
        out_shape=(
            jax.ShapeDtypeStruct((TOK, GROUP * HEAD), BF16),
            jax.ShapeDtypeStruct((2 * TOK, width), BF16),
            jax.ShapeDtypeStruct((2 * TOK, width), F32),
            jax.ShapeDtypeStruct((TOK, width), F32),
        ),
        in_specs=[SMEM] + [VMEM] * 5,
        out_specs=(VMEM,) * 4,
        scratch_shapes=[
            pltpu.VMEM((8, TOK), F32),
            pltpu.VMEM((HEAD, (REACH + 1) * TOK), BF16),
            pltpu.VMEM((REACH + 1, TOK, width), F32),
        ],
        cost_estimate=pl.CostEstimate(flops=2_600_000_000, bytes_accessed=4_000_000, transcendentals=2_000_000),
        compiler_params=pltpu.CompilerParams(vmem_limit_bytes=24 << 20),
        name="attention",
    )(frame_lists, qg, kv0, kv13, kv2, kv4)
    came = shifted(send, -1).astype(F32) + keep
    came = came.astype(BF16)
    far = shifted(came[:TOK], -3)
    near = shifted(came[TOK:], -1)
    total = own + far.astype(F32) + near.astype(F32)
    return dq, total[:, :HEAD].astype(BF16), total[:, HEAD:].astype(BF16)


def solution(mesh):
    both = P(("ctx", "head"), None)
    return jax.shard_map(
        on_device,
        mesh=mesh,
        in_specs=(both,) * 5 + (P("ctx", None),),
        out_specs=(P("ctx", "head"),) * 3,
        check_vma=False,
    )
```

time: 220 us -> 96.4 us (0.44); the launches traced: 216 us -> 95.9 us
  starting transfers between devices: 104 us -> 29.9 us
  matrix products: 27.4 us -> 0 us
  Pallas kernels: 0 us -> 13.7 us
  waiting for transfers between devices: 59.8 us -> 47 us
  local copies, waits for them, and re-layouts: 14.4 us -> 4.4 us
  other arithmetic: 9.48 us -> 0.12 us
    ppermute x16 -> x6, starting transfers between devices: 83.3 us -> 22.1 us  [shifted(): lax.ppermute(value, 'ctx', [(s, s + steps) for s in range(first, last)])]
    dot_general x30 -> x0, matrix products: 27.4 us -> none  [the longest x6 13.4 us: one_head(): lax.dot_general(probability_block, grad_h, contract_first, preferred_elem...]
    all_to_all x5 -> x2, waiting for transfers between devices: 20.4 us -> 2.9 us  [regroup(): lax.all_to_all(value, 'head', split_axis=0, concat_axis=0, tiled=True)]
    pallas_call x0 -> x3, Pallas kernels: none -> 13.7 us  [the longest x1 11.8 us: on_device(): pl.pallas_call(attention_kernel, out_shape=(jax.ShapeDtypeStruct((TOK, GR...]
    all_to_all x5 -> x2, starting transfers between devices: 20.3 us -> 7.85 us  [regroup(): lax.all_to_all(value, 'head', split_axis=0, concat_axis=0, tiled=True)]
    reduce_sum x9 -> x0, other arithmetic: 7.24 us -> none  [the longest x1 2.42 us: on_device(): key_sum = key_terms_all.reshape(kv_count, query_group_width, key_extent,...]
    all_to_all x5 -> x0, local copies, waits for them, and re-layouts: 5.58 us -> none  [the longest x1 1.82 us: on_device(): lax.all_to_all(queries, 'head', split_axis=1, concat_axis=0, tiled=True)]
    ppermute x16 -> x6, waiting for transfers between devices: 39.4 us -> 44.1 us  [shifted(): lax.ppermute(value, 'ctx', [(s, s + steps) for s in range(first, last)])]
  transfers between devices with their start and end apart: 21 -> 8, of which waited for: 10 -> 6; matrix products, arithmetic and copies ran while one was open for 3% -> 0% of each run, Pallas kernels for 0% -> 1%
where the time goes in v1:
time: 96.4 us; the launch traced here: 95.9 us
  waiting for transfers between devices  47 us (49%)
  starting transfers between devices  29.9 us (31%)
  Pallas kernels  13.7 us (14%)
  local copies, waits for them, and re-layouts  4.4 us (5%)
    ppermute x6, waiting for transfers between devices, shifted(): lax.ppermute(value, 'ctx', [(s, s + steps) for s in range(first, last)])  44.1 us
    ppermute x6, starting transfers between devices, shifted(): lax.ppermute(value, 'ctx', [(s, s + steps) for s in range(first, last)])  22.1 us
    pallas_call x1, Pallas kernels, on_device(): pl.pallas_call(attention_kernel, out_shape=(jax.ShapeDtypeStruct((TOK, GR...  11.8 us
    all_to_all x2, starting transfers between devices, regroup(): lax.all_to_all(value, 'head', split_axis=0, concat_axis=0, tiled=True)  7.85 us
    unnamed x12, local copies, waits for them, and re-layouts  3.72 us
    all_to_all x2, waiting for transfers between devices, regroup(): lax.all_to_all(value, 'head', split_axis=0, concat_axis=0, tiled=True)  2.9 us
  transfers between devices with their start and end apart: 8, of which 6 were waited for; matrix products, arithmetic and copies ran while one was open for 0% of the time, Pallas kernels for 1%

profile of v1, /device:TPU:24, one launch (start us, length us, event | category | flops | bytes accessed | tf_op | source)
XLA Modules:
  0.0 95.9 jit_solution(13304167180192477795)
XLA Ops:
  0.6 0.0 copy-start
  0.6 0.0 copy-start.3
  0.7 0.9 copy-done.3
  1.5 0.0 copy-start.4
  1.5 0.8 copy-done.4
  2.4 0.7 pack_kv.1
  3.0 4.3 %all-to-all-start.1 = ((bf16[8,32,256]{2,1,0:T(8,128)(2,1)}), bf16[8,32,256]{2,1,0:T(8,128)(2,1)S(1)}, u32[]{:S(2)}, u32[]{:S(2)}) async-start(bf16[8,32,256]{2,1,0:T(8,128)(2,1)} %pack_kv.1), calls=%async_computation.1 | async-start | bytes 262144 | tf_op jit(solution)/shard_map/all_to_all | solution.py:32
  7.3 0.0 copy-done
  7.4 0.0 copy-start.1
  7.4 1.0 %copy-done.1 = bf16[32,6144]{1,0:T(8,128)(2,1)S(1)} copy-done((bf16[32,6144]{1,0:T(8,128)(2,1)S(1)}, bf16[32,6144]{1,0:T(8,128)(2,1)}, u32[]{:S(2)}) %copy-start.1) | copy-done | bytes 393240
  8.4 1.0 %copy-done.2 = bf16[32,6144]{1,0:T(8,128)(2,1)S(1)} copy-done((bf16[32,6144]{1,0:T(8,128)(2,1)S(1)}, bf16[32,6144]{1,0:T(8,128)(2,1)}, u32[]{:S(2)}) %copy-start.2) | copy-done | bytes 393240
  9.4 1.2 %pack_qg.1 = bf16[8,32,1664]{2,1,0:T(8,128)(2,1)} custom-call(bf16[32,6144]{1,0:T(8,128)(2,1)S(1)} %copy-done, bf16[32,6144]{1,0:T(8,128)(2,1)S(1)} %copy-done.1, bf16[32,6144]{1,0:T(8,128)(2,1)S(1)} %copy-done.2), custom_call_target="tpu_custom_call" | custom-call | flops 1000000 | bytes 3000000 | tf_op jit(solution)/shard_map/pack_qg/pallas_call | solution.py:131
  10.6 2.9 %all-to-all-done.1 = bf16[8,32,256]{2,1,0:T(8,128)(2,1)S(1)} async-done(((bf16[8,32,256]{2,1,0:T(8,128)(2,1)}), bf16[8,32,256]{2,1,0:T(8,128)(2,1)S(1)}, u32[]{:S(2)}, u32[]{:S(2)}) %all-to-all-start.1) | async-done | bytes 131104 | tf_op jit(solution)/shard_map/all_to_all | solution.py:32
  13.5 3.5 %all-to-all-start = ((bf16[8,32,1664]{2,1,0:T(8,128)(2,1)}), bf16[8,32,1664]{2,1,0:T(8,128)(2,1)S(1)}, u32[]{:S(2)}, u32[]{:S(2)}) async-start(bf16[8,32,1664]{2,1,0:T(8,128)(2,1)} %pack_qg.1), calls=%async_computation | async-start | bytes 1703936 | tf_op jit(solution)/shard_map/all_to_all | solution.py:32
  17.0 5.2 %collective-permute-start = (bf16[256,256]{1,0:T(8,128)(2,1)S(1)}, bf16[256,256]{1,0:T(8,128)(2,1)S(1)}, u32[]{:S(2)}, u32[]{:S(2)}) collective-permute-start(bf16[256,256]{1,0:T(8,128)(2,1)S(1)} %bitcast.3), channel_id=1, source_target_pairs={{0,16},{8,24},{16,32},{24,40},{32,48},{40,56},{48,64},{56,72},{64,... | collective-permute-start | bytes 393224 | tf_op jit(solution)/shard_map/ppermute | solution.py:28
  22.2 18.7 %collective-permute-done.kv2_ref = bf16[256,256]{1,0:T(8,128)(2,1)S(1)} collective-permute-done((bf16[256,256]{1,0:T(8,128)(2,1)S(1)}, bf16[256,256]{1,0:T(8,128)(2,1)S(1)}, u32[]{:S(2)}, u32[]{:S(2)}) %collective-permute-start) | collective-permute-done | bytes 131104 | tf_op jit(solution)/shard_map/ppermute | solution.py:28
  41.0 0.0 copy-start.5
  41.0 5.1 %collective-permute-start.1 = (bf16[512,256]{1,0:T(8,128)(2,1)S(1)}, bf16[512,256]{1,0:T(8,128)(2,1)S(1)}, u32[]{:S(2)}, u32[]{:S(2)}) collective-permute-start(bf16[512,256]{1,0:T(8,128)(2,1)S(1)} %pad_maximum_fusion), channel_id=1, source_target_pairs={{0,8},{8,16},{16,24},{24,32},{32,40},{40,48},{48,56},{56,64},{64,7... | collective-permute-start | bytes 786440 | tf_op jit(solution)/shard_map/ppermute | solution.py:28
  46.1 1.9 %collective-permute-start.2 = (bf16[256,256]{1,0:T(8,128)(2,1)S(1)}, bf16[256,256]{1,0:T(8,128)(2,1)S(1)}, u32[]{:S(2)}, u32[]{:S(2)}) collective-permute-start(bf16[256,256]{1,0:T(8,128)(2,1)S(1)} %collective-permute-done.kv2_ref), channel_id=1, source_target_pairs={{0,16},{8,24},{16,32},{24,40},{32,48},{40,56},{48,64},{56,72},{64,... | collective-permute-start | bytes 393224 | tf_op jit(solution)/shard_map/ppermute | solution.py:28
  48.1 12.1 %collective-permute-done.2.kv4_ref = bf16[256,256]{1,0:T(8,128)(2,1)S(1)} collective-permute-done((bf16[256,256]{1,0:T(8,128)(2,1)S(1)}, bf16[256,256]{1,0:T(8,128)(2,1)S(1)}, u32[]{:S(2)}, u32[]{:S(2)}) %collective-permute-start.2) | collective-permute-done | bytes 131104 | tf_op jit(solution)/shard_map/ppermute | solution.py:28
  60.1 0.0 collective-permute-done.1.kv13_ref
  60.1 0.0 all-to-all-done
  60.1 0.0 copy-done.5
  60.1 11.8 %attention.1 = (bf16[256,768]{1,0:T(8,128)(2,1)}, bf16[512,256]{1,0:T(8,128)(2,1)S(1)}, f32[512,256]{1,0:T(8,128)S(1)}, f32[256,256]{1,0:T(8,128)S(1)}) custom-call(s32[1,5]{1,0:T(1,128)S(1)} %copy-done.5, bf16[256,1664]{1,0:T(8,128)(2,1)S(1)} %bitcast.2, bf16[256,256]{1,0:T(8,128)(2,1)S(1)} %bitcast.5, ...), custom_call_target="tpu_custom_call" | custom-call | flops 2600000000 | bytes 4000000 | tf_op jit(solution)/shard_map/attention/pallas_call | solution.py:146
  71.9 1.9 %collective-permute-start.3 = (bf16[512,256]{1,0:T(8,128)(2,1)S(1)}, bf16[512,256]{1,0:T(8,128)(2,1)S(1)}, u32[]{:S(2)}, u32[]{:S(2)}) collective-permute-start(bf16[512,256]{1,0:T(8,128)(2,1)S(1)} %get-tuple-element.9), channel_id=1, source_target_pairs={{8,0},{16,8},{24,16},{32,24},{40,32},{48,40},{56,48},{64,56},{72,6... | collective-permute-start | bytes 786440 | tf_op jit(solution)/shard_map/ppermute | solution.py:28
  73.9 6.3 %collective-permute-done.3 = bf16[512,256]{1,0:T(8,128)(2,1)S(1)} collective-permute-done((bf16[512,256]{1,0:T(8,128)(2,1)S(1)}, bf16[512,256]{1,0:T(8,128)(2,1)S(1)}, u32[]{:S(2)}, u32[]{:S(2)}) %collective-permute-start.3) | collective-permute-done | bytes 262176 | tf_op jit(solution)/shard_map/ppermute | solution.py:28
  80.2 0.1 add_convert_fusion
  80.3 4.1 %collective-permute-start.4 = (bf16[256,256]{1,0:T(8,128)(2,1)S(1)}, bf16[256,256]{1,0:T(8,128)(2,1)S(1)}, u32[]{:S(2)}, u32[]{:S(2)}) collective-permute-start(bf16[256,256]{1,0:T(8,128)(2,1)S(1)} %get-tuple-element.11), channel_id=1, source_target_pairs={{24,0},{32,8},{40,16},{48,24},{56,32},{64,40},{72,48},{80,56},{88,... | collective-permute-start | bytes 393224 | tf_op jit(solution)/shard_map/ppermute | solution.py:28
  84.4 3.8 %collective-permute-start.5 = (bf16[256,256]{1,0:T(8,128)(2,1)S(1)}, bf16[256,256]{1,0:T(8,128)(2,1)S(1)}, u32[]{:S(2)}, u32[]{:S(2)}) collective-permute-start(bf16[256,256]{1,0:T(8,128)(2,1)S(1)} %get-tuple-element.12), channel_id=1, source_target_pairs={{8,0},{16,8},{24,16},{32,24},{40,32},{48,40},{56,48},{64,56},{72,6... | collective-permute-start | bytes 393224 | tf_op jit(solution)/shard_map/ppermute | solution.py:28
  88.2 3.5 %collective-permute-done.4 = bf16[256,256]{1,0:T(8,128)(2,1)S(1)} collective-permute-done((bf16[256,256]{1,0:T(8,128)(2,1)S(1)}, bf16[256,256]{1,0:T(8,128)(2,1)S(1)}, u32[]{:S(2)}, u32[]{:S(2)}) %collective-permute-start.4) | collective-permute-done | bytes 131104 | tf_op jit(solution)/shard_map/ppermute | solution.py:28
  91.8 3.4 %collective-permute-done.5 = bf16[256,256]{1,0:T(8,128)(2,1)S(1)} collective-permute-done((bf16[256,256]{1,0:T(8,128)(2,1)S(1)}, bf16[256,256]{1,0:T(8,128)(2,1)S(1)}, u32[]{:S(2)}, u32[]{:S(2)}) %collective-permute-start.5) | collective-permute-done | bytes 131104 | tf_op jit(solution)/shard_map/ppermute | solution.py:28
  95.2 0.7 fusion.1
  (4 shorter events, 0.1 us)
Async XLA Ops:
  0.6 6.7 %copy-start = (bf16[32,6144]{1,0:T(8,128)(2,1)S(1)}, bf16[32,6144]{1,0:T(8,128)(2,1)}, u32[]{:S(2)}) copy-start(bf16[32,6144]{1,0:T(8,128)(2,1)} %q_ref.1) | copy-start | bytes 1179652
  0.6 0.9 copy-start.3
  1.5 0.8 copy-start.4
  3.0 10.4 %all-to-all-start.1 = ((bf16[8,32,256]{2,1,0:T(8,128)(2,1)}), bf16[8,32,256]{2,1,0:T(8,128)(2,1)S(1)}, u32[]{:S(2)}, u32[]{:S(2)}) async-start(bf16[8,32,256]{2,1,0:T(8,128)(2,1)} %pack_kv.1), calls=%async_computation.1 | async-start | bytes 262144 | tf_op jit(solution)/shard_map/all_to_all | solution.py:32
  7.4 1.0 %copy-start.1 = (bf16[32,6144]{1,0:T(8,128)(2,1)S(1)}, bf16[32,6144]{1,0:T(8,128)(2,1)}, u32[]{:S(2)}) copy-start(bf16[32,6144]{1,0:T(8,128)(2,1)} %g_ref.1) | copy-start | bytes 1179652
  8.4 1.0 %copy-start.2 = (bf16[32,6144]{1,0:T(8,128)(2,1)S(1)}, bf16[32,6144]{1,0:T(8,128)(2,1)}, u32[]{:S(2)}) copy-start(bf16[32,6144]{1,0:T(8,128)(2,1)} %o_ref.1) | copy-start | bytes 1179652
  13.5 46.7 %all-to-all-start = ((bf16[8,32,1664]{2,1,0:T(8,128)(2,1)}), bf16[8,32,1664]{2,1,0:T(8,128)(2,1)S(1)}, u32[]{:S(2)}, u32[]{:S(2)}) async-start(bf16[8,32,1664]{2,1,0:T(8,128)(2,1)} %pack_qg.1), calls=%async_computation | async-start | bytes 1703936 | tf_op jit(solution)/shard_map/all_to_all | solution.py:32
  17.0 23.9 %collective-permute-start = (bf16[256,256]{1,0:T(8,128)(2,1)S(1)}, bf16[256,256]{1,0:T(8,128)(2,1)S(1)}, u32[]{:S(2)}, u32[]{:S(2)}) collective-permute-start(bf16[256,256]{1,0:T(8,128)(2,1)S(1)} %bitcast.3), channel_id=1, source_target_pairs={{0,16},{8,24},{16,32},{24,40},{32,48},{40,56},{48,64},{56,72},{64,... | collective-permute-start | bytes 393224 | tf_op jit(solution)/shard_map/ppermute | solution.py:28
  41.0 19.2 %copy-start.5 = (s32[1,5]{1,0:T(1,128)S(1)}, s32[1,5]{1,0:T(1,128)}, u32[]{:S(2)}) copy-start(s32[1,5]{1,0:T(1,128)} %lists_ref.1) | copy-start | bytes 64
  41.0 19.1 %collective-permute-start.1 = (bf16[512,256]{1,0:T(8,128)(2,1)S(1)}, bf16[512,256]{1,0:T(8,128)(2,1)S(1)}, u32[]{:S(2)}, u32[]{:S(2)}) collective-permute-start(bf16[512,256]{1,0:T(8,128)(2,1)S(1)} %pad_maximum_fusion), channel_id=1, source_target_pairs={{0,8},{8,16},{16,24},{24,32},{32,40},{40,48},{48,56},{56,64},{64,7... | collective-permute-start | bytes 786440 | tf_op jit(solution)/shard_map/ppermute | solution.py:28
  46.1 14.0 %collective-permute-start.2 = (bf16[256,256]{1,0:T(8,128)(2,1)S(1)}, bf16[256,256]{1,0:T(8,128)(2,1)S(1)}, u32[]{:S(2)}, u32[]{:S(2)}) collective-permute-start(bf16[256,256]{1,0:T(8,128)(2,1)S(1)} %collective-permute-done.kv2_ref), channel_id=1, source_target_pairs={{0,16},{8,24},{16,32},{24,40},{32,48},{40,56},{48,64},{56,72},{64,... | collective-permute-start | bytes 393224 | tf_op jit(solution)/shard_map/ppermute | solution.py:28
  71.9 8.3 %collective-permute-start.3 = (bf16[512,256]{1,0:T(8,128)(2,1)S(1)}, bf16[512,256]{1,0:T(8,128)(2,1)S(1)}, u32[]{:S(2)}, u32[]{:S(2)}) collective-permute-start(bf16[512,256]{1,0:T(8,128)(2,1)S(1)} %get-tuple-element.9), channel_id=1, source_target_pairs={{8,0},{16,8},{24,16},{32,24},{40,32},{48,40},{56,48},{64,56},{72,6... | collective-permute-start | bytes 786440 | tf_op jit(solution)/shard_map/ppermute | solution.py:28
  80.3 11.5 %collective-permute-start.4 = (bf16[256,256]{1,0:T(8,128)(2,1)S(1)}, bf16[256,256]{1,0:T(8,128)(2,1)S(1)}, u32[]{:S(2)}, u32[]{:S(2)}) collective-permute-start(bf16[256,256]{1,0:T(8,128)(2,1)S(1)} %get-tuple-element.11), channel_id=1, source_target_pairs={{24,0},{32,8},{40,16},{48,24},{56,32},{64,40},{72,48},{80,56},{88,... | collective-permute-start | bytes 393224 | tf_op jit(solution)/shard_map/ppermute | solution.py:28
  84.4 10.8 %collective-permute-start.5 = (bf16[256,256]{1,0:T(8,128)(2,1)S(1)}, bf16[256,256]{1,0:T(8,128)(2,1)S(1)}, u32[]{:S(2)}, u32[]{:S(2)}) collective-permute-start(bf16[256,256]{1,0:T(8,128)(2,1)S(1)} %get-tuple-element.12), channel_id=1, source_target_pairs={{8,0},{16,8},{24,16},{32,24},{40,32},{48,40},{56,48},{64,56},{72,6... | collective-permute-start | bytes 393224 | tf_op jit(solution)/shard_map/ppermute | solution.py:28
